TPU v7x, 256 devices: a whole 4x4x8 slice. The times are simulated.
256 devices in a mesh: tp: 2 (over z_lo), sp: 32 (over x, y, core), dp: 4 (over z_hi).
Axes of the slice: x: 4, y: 4, z: 8 (z_hi: 4, z_lo: 2; z = z_hi * 2 + z_lo), core: 2. Of those that a mesh axis runs over, the one named last changes fastest.
Arguments:
- queries: bfloat16 [16384, 4096], P(('dp', 'sp'), 'tp'), parts along dimension 0, may hold values from -256 to 256
- key_projection_rows: bfloat16 [16384, 512], P(('dp', 'sp'), 'tp'), parts along dimension 0, may hold values from -8 to 8
- values: bfloat16 [16384, 512], P(('dp', 'sp'), 'tp'), parts along dimension 0, may hold values from -6 to 6
- segment_ids: int32 [16384], P('dp'), parts along dimension 0, may hold values from 0 to 11, never falling along the last dimension, each value on 1 to 1024 neighbouring positions
- residual: bfloat16 [16384, 8192], P(('dp', 'tp'), 'sp'), parts along dimension 0, may hold values from -40 to 40
- out_weight: bfloat16 [4096, 8192], P('tp', 'sp'), may hold values from -0.09375 to 0.09375
- norm_gain: float32 [8192], P('sp'), may hold values from 0.1 to 1.9
- scale_exponent: int32 [8192], P('sp'), may hold values from 7 to 8
Outputs:
- hidden_out: bfloat16 [16384, 8192], P(('dp', 'tp'), 'sp'), parts along dimension 0
- quantized: bfloat16 [16384, 8192], P(('dp', 'tp'), 'sp'), parts along dimension 0
There are 4 independent parts, one for each index of `dp`. A program takes and returns all parts, laid end to end along the dimension named above; an argument that names none is the same for every part. Nothing has to cross between parts.
Inputs may be any that keep to these rules, and one draw needn't show every extreme that they name: `segment_ids`: never falls along the window; every document holds at most a quarter of the window's tokens, and one holds exactly that many.
All inputs are finite; a program needn't handle non-finite values.
Results may differ from a plain program's by a relative error of at most 0.0065.
Values may be sent and summed in bfloat16 or wider, within the bound.
No kernel may reach another device: no remote copies, remote signals or barrier semaphores. Data moves between devices by JAX's collectives and lax.ppermute only.
A program may use at most 64 MiB of HBM per device.

v0:
```python
import jax
import jax.numpy as jnp
from jax import lax
from jax.sharding import PartitionSpec as P

D = 8192
QUERY_HEAD_COUNT = 32
KEY_VALUE_HEADS = 4
HEAD_DIMENSION = 128
epsilon = 1e-05
limit_value = 448.0


def attend_item(query_block, key_block, value_block, query_pos, query_seg, segment_ids, key_pos):
    query_count = query_block.shape[0]
    block_rows = min(512, query_count)
    blocks = query_count // block_rows

    def one_block(packed):
        block_query, block_pos, block_seg = packed
        scores = lax.dot_general(
            block_query, key_block, (((1,), (1,)), ((), ())), preferred_element_type=jnp.float32
        ) * HEAD_DIMENSION ** (-0.5)
        visible = (key_pos[None, :] <= block_pos[:, None]) & (
            segment_ids[None, :] == block_seg[:, None]
        )
        scores = jnp.where(visible, scores, -1e30)
        largest = jnp.max(scores, axis=1, keepdims=True)
        weights = jnp.exp(scores - largest)
        row_total = jnp.sum(weights, axis=1, keepdims=True)
        probabilities = (weights / row_total).astype(jnp.bfloat16)
        return jnp.dot(probabilities, value_block, preferred_element_type=jnp.float32).astype(
            jnp.bfloat16
        )

    results = lax.map(
        one_block,
        (
            query_block.reshape(blocks, block_rows, HEAD_DIMENSION),
            query_pos.reshape(blocks, block_rows),
            query_seg.reshape(blocks, block_rows),
        ),
    )
    return results.reshape(query_count, HEAD_DIMENSION)


def body(
    queries,
    key_projection_rows,
    values,
    segment_ids,
    residual,
    out_weight,
    norm_gain,
    scale_exponent,
):
    sp_count = lax.axis_size("sp")
    token_rows = queries.shape[0]
    half_rows = token_rows // 2
    local_heads = queries.shape[1] // HEAD_DIMENSION
    item_count = 2 * local_heads
    per_device = item_count // sp_count
    window_token_rows = token_rows * sp_count
    query_count = window_token_rows // 2
    group_width = QUERY_HEAD_COUNT // KEY_VALUE_HEADS
    own_index = lax.axis_index("sp")
    query_items = jnp.transpose(
        queries.reshape(2, half_rows, local_heads, HEAD_DIMENSION), (0, 2, 1, 3)
    ).reshape(item_count, half_rows, HEAD_DIMENSION)
    query_recv = lax.all_to_all(query_items, "sp", split_axis=0, concat_axis=1, tiled=True)
    key_all, value_all = (
        lax.all_gather(key_projection_rows, "sp", axis=0, tiled=True),
        lax.all_gather(values, "sp", axis=0, tiled=True),
    )
    key_pos = jnp.arange(window_token_rows, dtype=jnp.int32)
    row_number = jnp.arange(query_count, dtype=jnp.int32)
    source_device = row_number // half_rows
    within = row_number % half_rows
    segment_grid = segment_ids.reshape(sp_count, 2, half_rows)
    number = 0
    item_index = own_index * per_device + number
    which_half = item_index // local_heads
    query_pos = source_device * token_rows + which_half * half_rows + within
    query_seg = lax.dynamic_index_in_dim(segment_grid, which_half, 1, keepdims=False).reshape(
        query_count
    )
    shared_rows = item_index % local_heads // group_width
    key_block = lax.dynamic_slice_in_dim(key_all, shared_rows * HEAD_DIMENSION, HEAD_DIMENSION, 1)
    value_block = lax.dynamic_slice_in_dim(
        value_all, shared_rows * HEAD_DIMENSION, HEAD_DIMENSION, 1
    )
    outputs = [
        attend_item(
            query_recv[number], key_block, value_block, query_pos, query_seg, segment_ids, key_pos
        )
    ]
    own_outputs = jnp.stack(outputs)
    column_count = out_weight.shape[1]
    start_sum = jnp.zeros((sp_count, 2, half_rows, column_count), jnp.float32)
    pieces = lax.all_gather(own_outputs, "sp", axis=0, tiled=True)

    def add_one(number, current):
        head_number = number % local_heads
        which_half = number // local_heads
        head_weight = lax.dynamic_slice_in_dim(
            out_weight, head_number * HEAD_DIMENSION, HEAD_DIMENSION, 0
        )
        chosen = lax.dynamic_index_in_dim(pieces, number, 0, keepdims=False)
        product_term = jnp.dot(chosen, head_weight, preferred_element_type=jnp.float32).reshape(
            sp_count, 1, half_rows, column_count
        )
        corner = (0, which_half, 0, 0)
        earlier = lax.dynamic_slice(current, corner, (sp_count, 1, half_rows, column_count))
        return lax.dynamic_update_slice(current, earlier + product_term, corner)

    combined = lax.fori_loop(0, pieces.shape[0], add_one, start_sum)
    flattened = combined.reshape(window_token_rows, column_count)
    share_rows = window_token_rows // lax.axis_size("tp")
    whole_sum = lax.psum(flattened, "tp")
    summed = lax.dynamic_slice_in_dim(whole_sum, lax.axis_index("tp") * share_rows, share_rows, 0)
    projected = summed.astype(jnp.bfloat16)
    hidden_out = (residual.astype(jnp.float32) + projected.astype(jnp.float32)).astype(jnp.bfloat16)
    widened = hidden_out.astype(jnp.float32)
    square_sum = lax.psum(jnp.sum(widened * widened, axis=1), "sp")
    mean_square = (square_sum / D)[:, None]
    normed = widened * lax.rsqrt(mean_square + epsilon) * norm_gain[None, :]
    clip_bound = (limit_value * jnp.exp2(-scale_exponent.astype(jnp.float32)))[None, :]
    quantized = jnp.clip(normed, -clip_bound, clip_bound).astype(jnp.bfloat16)
    return (hidden_out, quantized)


def solution(mesh):
    in_specs = (
        P(("dp", "sp"), "tp"),
        P(("dp", "sp"), "tp"),
        P(("dp", "sp"), "tp"),
        P("dp"),
        P(("dp", "tp"), "sp"),
        P("tp", "sp"),
        P("sp"),
        P("sp"),
    )
    out_specs = (P(("dp", "tp"), "sp"), P(("dp", "tp"), "sp"))
    return jax.shard_map(body, mesh=mesh, in_specs=in_specs, out_specs=out_specs, check_vma=False)
```

profile of v0, /device:TPU:1, one launch (start us, length us, event | category | flops | bytes accessed | tf_op | source)
XLA Modules:
  0.0 569.2 jit_solution(7606608849317972235)
XLA Ops:
  10.8 8.6 %all-to-all-start = ((bf16[32,64,128]{2,1,0:T(8,128)(2,1)}), bf16[32,64,128]{2,1,0:T(8,128)(2,1)S(1)}, u32[]{:S(2)}, u32[]{:S(2)}) async-start(bf16[32,64,128]{2,1,0:T(8,128)(2,1)} %bitcast.4), calls=%async_computation | async-start | bytes 1048576 | tf_op jit(solution)/shard_map/all_to_all | solution.py:70
  19.8 43.6 %all-gather.6.cloned.1.call-done = bf16[4096,256]{1,0:T(8,128)(2,1)} async-done(((bf16[128,256]{1,0:T(8,128)(2,1)}), bf16[4096,256]{1,0:T(8,128)(2,1)}) %all-gather.6.cloned.1.call-update) | async-done | bytes 2097168 | tf_op jit(solution)/shard_map/all_gather | solution.py:73
  64.6 49.3 %all-gather.4.cloned.1.call-done = bf16[4096,256]{1,0:T(8,128)(2,1)} async-done(((bf16[128,256]{1,0:T(8,128)(2,1)}), bf16[4096,256]{1,0:T(8,128)(2,1)}) %all-gather.4.cloned.1.call-update) | async-done | bytes 2097168 | tf_op jit(solution)/shard_map/all_gather | solution.py:72
  115.2 24.3 %while.27 = (s32[]{:T(128)}, bf16[4,512,128]{2,1,0:T(8,128)(2,1)S(1)}, s32[4,512]{1,0:T(4,128)S(1)}, s32[4096]{0:T(1024)S(1)}, s32[4,512]{1,0:T(4,128)S(1)}, /*i...) while((s32[]{:T(128)}, ...), condition=%wide.region_3.4_spmd.clone, body=%wide.region_0.3_spmd.clone.sunk | while | flops 1096875008 | bytes 27564136 | solution.py:36
  115.2 2.5 fusion.40
  121.3 2.5 fusion.40
  125.1 2.2 fusion.42
  127.4 2.5 fusion.40
  131.2 2.2 fusion.42
  133.4 2.5 fusion.40
  137.2 2.2 fusion.42
  140.3 77.1 %all-gather.8.cloned.1.call-done = bf16[32,2048,128]{2,1,0:T(8,128)(2,1)} async-done(((bf16[1,2048,128]{2,1,0:T(8,128)(2,1)}), bf16[32,2048,128]{2,1,0:T(8,128)(2,1)}) %all-gather.8.cloned.1.call-update) | async-done | bytes 16777232 | tf_op jit(solution)/shard_map/all_gather | solution.py:100
  217.4 2.4 broadcast_in_dim.18.clone
  219.9 174.8 %while.26 = (s32[]{:T(128)}, f32[32,2,64,256]{3,2,1,0:T(8,128)}, bf16[32,2048,128]{2,1,0:T(8,128)(2,1)}, bf16[2048,256]{1,0:T(8,128)(2,1)}, s32[]{:T(128)}, /*in...) while((s32[]{:T(128)}, f32[32,2,64,256]{3,2,1,0:T(8,128)}, ...), condition=%wide.region_5.6_spmd, body=%wide.region_4.5_spmd.sunk | while | flops 134742032 | bytes 10027344 | solution.py:116
  222.7 2.6 bitcast_dynamic-update-slice_fusion.2
  228.1 2.6 bitcast_dynamic-update-slice_fusion.2
  233.6 2.6 bitcast_dynamic-update-slice_fusion.2
  239.0 2.6 bitcast_dynamic-update-slice_fusion.2
  244.4 2.6 bitcast_dynamic-update-slice_fusion.2
  249.9 2.6 bitcast_dynamic-update-slice_fusion.2
  255.3 2.6 bitcast_dynamic-update-slice_fusion.2
  260.7 2.6 bitcast_dynamic-update-slice_fusion.2
  266.1 2.6 bitcast_dynamic-update-slice_fusion.2
  271.6 2.6 bitcast_dynamic-update-slice_fusion.2
  277.0 2.6 bitcast_dynamic-update-slice_fusion.2
  282.4 2.6 bitcast_dynamic-update-slice_fusion.2
  287.9 2.6 bitcast_dynamic-update-slice_fusion.2
  293.3 2.6 bitcast_dynamic-update-slice_fusion.2
  298.7 2.6 bitcast_dynamic-update-slice_fusion.2
  304.1 2.6 bitcast_dynamic-update-slice_fusion.2
  309.6 2.6 bitcast_dynamic-update-slice_fusion.2
  315.1 2.6 bitcast_dynamic-update-slice_fusion.2
  320.6 2.6 bitcast_dynamic-update-slice_fusion.2
  326.0 2.6 bitcast_dynamic-update-slice_fusion.2
  331.5 2.6 bitcast_dynamic-update-slice_fusion.2
  337.0 2.6 bitcast_dynamic-update-slice_fusion.2
  342.5 2.6 bitcast_dynamic-update-slice_fusion.2
  348.0 2.6 bitcast_dynamic-update-slice_fusion.2
  353.5 2.6 bitcast_dynamic-update-slice_fusion.2
  359.0 2.6 bitcast_dynamic-update-slice_fusion.2
  364.5 2.6 bitcast_dynamic-update-slice_fusion.2
  370.0 2.6 bitcast_dynamic-update-slice_fusion.2
  375.5 2.6 bitcast_dynamic-update-slice_fusion.2
  381.0 2.6 bitcast_dynamic-update-slice_fusion.2
  386.5 2.6 bitcast_dynamic-update-slice_fusion.2
  392.0 2.6 bitcast_dynamic-update-slice_fusion.2
  394.7 100.2 %all-reduce.1 = bf16[4096,256]{1,0:T(8,128)(2,1)S(1)} all-reduce(f32[4096,256]{1,0:T(8,128)} %bitcast.61), channel_id=1, replica_groups=mesh['tp'=2,'sp'=32,'dp'=4] {'tp'}, use_global_device_ids=true, to_apply=%region_6.7 | all-reduce | flops 1048576 | bytes 6291456 | tf_op jit(solution)/shard_map/psum | solution.py:119
  496.6 64.7 %psum.15 = f32[2048]{0:T(1024)S(1)} all-reduce(f32[2048]{0:T(1024)S(1)} %get-tuple-element.206), channel_id=1, replica_groups=mesh['tp'=2,'sp'=32,'dp'=4] {'sp'}, use_global_device_ids=true, to_apply=%region_8.9 | all-reduce | flops 2048 | bytes 16384 | tf_op jit(solution)/shard_map/psum | solution.py:124
  (104 shorter events, 108.5 us)
Async XLA Ops:
  7.2 12.3 %copy-start.2 = (s32[4096]{0:T(1024)S(1)}, s32[4096]{0:T(1024)}, u32[]{:S(2)}) copy-start(s32[4096]{0:T(1024)} %param.15) | copy-start | bytes 49156
  7.2 56.2 %all-gather.6.cloned.1.call-start = ((), (), s32[]{:S(2)}) async-start(), calls=%async_computation.2 | async-start | bytes 2162688 | tf_op jit(solution)/shard_map/all_gather | solution.py:73
  7.9 106.0 %all-gather.4.cloned.1.call-start = ((), (), s32[]{:S(2)}) async-start(), calls=%async_computation.1 | async-start | bytes 2162688 | tf_op jit(solution)/shard_map/all_gather | solution.py:72
  10.8 104.4 %all-to-all-start = ((bf16[32,64,128]{2,1,0:T(8,128)(2,1)}), bf16[32,64,128]{2,1,0:T(8,128)(2,1)S(1)}, u32[]{:S(2)}, u32[]{:S(2)}) async-start(bf16[32,64,128]{2,1,0:T(8,128)(2,1)} %bitcast.4), calls=%async_computation | async-start | bytes 1048576 | tf_op jit(solution)/shard_map/all_to_all | solution.py:70
  19.4 198.0 %all-gather.8.cloned.1.call-start = ((), (), s32[]{:S(2)}) async-start(), calls=%async_computation.3 | async-start | bytes 17301504 | tf_op jit(solution)/shard_map/all_gather | solution.py:100
  115.2 25.1 %copy-start.4 = (s32[256]{0:T(256)S(1)}, s32[256]{0:T(256)}, u32[]{:S(2)}) copy-start(s32[256]{0:T(256)} %param.19) | copy-start | bytes 3076
  139.5 0.8 copy-start.1
  394.7 166.6 %copy-start.3 = (f32[256]{0:T(256)S(1)}, f32[256]{0:T(256)}, u32[]{:S(2)}) copy-start(f32[256]{0:T(256)} %param.18) | copy-start | bytes 3076
  496.5 66.2 %copy-start = (bf16[2048,256]{1,0:T(8,128)(2,1)}, bf16[2048,256]{1,0:T(8,128)(2,1)S(1)}, u32[]{:S(2)}) copy-start(bf16[2048,256]{1,0:T(8,128)(2,1)S(1)} %get-tuple-element.207) | copy-start | bytes 3145732
Sparse Core Ops, SparseCore 0:
  10.5 52.7 all-gather.5
  65.9 47.9 all-gather.3
  140.4 76.9 all-gather.7
where the time goes:
time: 574 us; the launch traced here: 569 us
  waiting for transfers between devices  171 us (30%)
  blocking collectives  165 us (29%)
  matrix products  103 us (18%)
  local copies, waits for them, and re-layouts  98.9 us (17%)
  between operations  14 us (2%)
  starting transfers between devices  8.69 us (2%)
  other arithmetic  8.28 us (1%)
    psum x1, blocking collectives, body(): whole_sum = lax.psum(flattened, 'tp')  100 us
    dot_general x32, matrix products, add_one(): jnp.dot(chosen, head_weight, preferred_element_type=jnp.float32)  83.6 us
    all_gather x1, waiting for transfers between devices, body(): pieces = lax.all_gather(own_outputs, 'sp', axis=0, tiled=True)  77.1 us
    psum x1, blocking collectives, body(): square_sum = lax.psum(jnp.sum(widened * widened, axis=1), 'sp')  64.7 us
    dynamic_slice x32, local copies, waits for them, and re-layouts, add_one(): lax.dynamic_slice(current, corner, (sp_count, 1, half_rows, column_count))  56.2 us
    all_gather x1, waiting for transfers between devices, body(): lax.all_gather(key_projection_rows, 'sp', axis=0, tiled=True)  49.3 us
    all_gather x1, waiting for transfers between devices, body(): lax.all_gather(values, 'sp', axis=0, tiled=True)  43.6 us
    dynamic_slice x32, local copies, waits for them, and re-layouts, add_one(): chosen = lax.dynamic_index_in_dim(pieces, number, 0, keepdims=False)  34.6 us
  transfers between devices with their start and end apart: 4, of which 3 were waited for; matrix products, arithmetic and copies ran while one was open for 1% of the time, Pallas kernels for 0%

commit v1 on v0

--- a/solution.py
+++ b/solution.py
@@ -9,6 +9,12 @@
 HEAD_DIMENSION = 128
 epsilon = 1e-05
 limit_value = 448.0
+
+
+def gather_from_all(x, axis, dim):
+    count = lax.axis_size(axis)
+    repeats = [count if d == dim else 1 for d in range(x.ndim)]
+    return lax.all_to_all(jnp.tile(x, repeats), axis, split_axis=dim, concat_axis=dim, tiled=True)
 
 
 def attend_item(query_block, key_block, value_block, query_pos, query_seg, segment_ids, key_pos):
@@ -70,7 +76,7 @@
     query_recv = lax.all_to_all(query_items, "sp", split_axis=0, concat_axis=1, tiled=True)
     key_all, value_all = (
         lax.all_gather(key_projection_rows, "sp", axis=0, tiled=True),
-        lax.all_gather(values, "sp", axis=0, tiled=True),
+        gather_from_all(values, "sp", 0),
     )
     key_pos = jnp.arange(window_token_rows, dtype=jnp.int32)
     row_number = jnp.arange(query_count, dtype=jnp.int32)

time: 574 us -> 542 us (0.944)
  waiting for transfers between devices: 171 us -> 127 us
  matrix products: 103 us -> 110 us
    all_gather x1 -> x0, waiting for transfers between devices: 43.6 us -> none  [body(): lax.all_gather(values, 'sp', axis=0, tiled=True)]
    all_gather x1, waiting for transfers between devices: 49.3 us -> 20 us  [body(): lax.all_gather(key_projection_rows, 'sp', axis=0, tiled=True)]
    all_to_all x0 -> x1, waiting for transfers between devices: none -> 27.8 us  [gather_from_all(): lax.all_to_all(jnp.tile(x, repeats), axis, split_axis=dim, concat_axis=di...]
    all_to_all x0 -> x1, starting transfers between devices: none -> 8.58 us  [gather_from_all(): lax.all_to_all(jnp.tile(x, repeats), axis, split_axis=dim, concat_axis=di...]
where the time goes in v1:
time: 542 us; the launch traced here: 537 us
  blocking collectives  165 us (30%)
  waiting for transfers between devices  127 us (23%)
  matrix products  110 us (20%)
  local copies, waits for them, and re-layouts  98.3 us (18%)
  between operations  14.3 us (3%)
  starting transfers between devices  13.7 us (3%)
  other arithmetic  8.25 us (2%)
    psum x1, blocking collectives, body(): whole_sum = lax.psum(flattened, 'tp')  100 us
    dot_general x32, matrix products, add_one(): jnp.dot(chosen, head_weight, preferred_element_type=jnp.float32)  84.7 us
    all_gather x1, waiting for transfers between devices, body(): pieces = lax.all_gather(own_outputs, 'sp', axis=0, tiled=True)  78.5 us
    psum x1, blocking collectives, body(): square_sum = lax.psum(jnp.sum(widened * widened, axis=1), 'sp')  64.7 us
    dynamic_slice x32, local copies, waits for them, and re-layouts, add_one(): lax.dynamic_slice(current, corner, (sp_count, 1, half_rows, column_count))  56.2 us
    dynamic_slice x32, local copies, waits for them, and re-layouts, add_one(): chosen = lax.dynamic_index_in_dim(pieces, number, 0, keepdims=False)  34.6 us
    all_to_all x1, waiting for transfers between devices, gather_from_all(): lax.all_to_all(jnp.tile(x, repeats), axis, split_axis=dim, concat_axis=di...  27.8 us
    all_gather x1, waiting for transfers between devices, body(): lax.all_gather(key_projection_rows, 'sp', axis=0, tiled=True)  20 us
  transfers between devices with their start and end apart: 4, of which 3 were waited for; matrix products, arithmetic and copies ran while one was open for 1% of the time, Pallas kernels for 0%

profile of v1, /device:TPU:1, one launch (start us, length us, event | category | flops | bytes accessed | tf_op | source)
XLA Modules:
  0.0 537.4 jit_solution(11160819682007191023)
XLA Ops:
  10.3 8.6 %all-to-all-start.1 = ((bf16[32,128,256]{2,1,0:T(8,128)(2,1)}), bf16[32,128,256]{2,1,0:T(8,128)(2,1)S(1)}, u32[]{:S(2)}, u32[]{:S(2)}) async-start(bf16[32,128,256]{2,1,0:T(8,128)(2,1)} %tile.2), calls=%async_computation.1 | async-start | bytes 4194304 | tf_op jit(solution)/shard_map/all_to_all | solution.py:17
  20.3 27.8 %all-to-all-done.1 = bf16[32,128,256]{2,1,0:T(8,128)(2,1)S(1)} async-done(((bf16[32,128,256]{2,1,0:T(8,128)(2,1)}), bf16[32,128,256]{2,1,0:T(8,128)(2,1)S(1)}, u32[]{:S(2)}, u32[]{:S(2)}) %all-to-all-start.1) | async-done | bytes 2097184 | tf_op jit(solution)/shard_map/all_to_all | solution.py:17
  48.2 5.0 all-to-all-start
  53.3 20.0 %all-gather.3.cloned.1.call-done = bf16[4096,256]{1,0:T(8,128)(2,1)} async-done(((bf16[128,256]{1,0:T(8,128)(2,1)}), bf16[4096,256]{1,0:T(8,128)(2,1)}) %all-gather.3.cloned.1.call-update) | async-done | bytes 2097168 | tf_op jit(solution)/shard_map/all_gather | solution.py:78
  74.7 31.0 %while.27 = (s32[]{:T(128)}, bf16[4,512,128]{2,1,0:T(8,128)(2,1)}, s32[4,512]{1,0:T(4,128)S(1)}, s32[4096]{0:T(1024)S(1)}, s32[4,512]{1,0:T(4,128)S(1)}, /*index...) while((s32[]{:T(128)}, bf16[4,512,128]{2,1,0:T(8,128)(2,1)}, ...), condition=%wide.region_3.4_spmd.clone, body=%wide.region_0.3_spmd.clone.sunk | while | flops 1096875008 | bytes 27565152 | solution.py:42
  74.7 3.6 fusion.40
  79.6 2.8 fusion.42
  82.4 3.6 fusion.40
  87.3 2.8 fusion.42
  90.2 3.6 fusion.40
  95.1 2.8 fusion.42
  97.9 3.6 fusion.40
  102.8 2.8 fusion.42
  105.7 78.5 %all-gather.5.cloned.1.call-done = bf16[32,2048,128]{2,1,0:T(8,128)(2,1)} async-done(((bf16[1,2048,128]{2,1,0:T(8,128)(2,1)}), bf16[32,2048,128]{2,1,0:T(8,128)(2,1)}) %all-gather.5.cloned.1.call-update) | async-done | bytes 16777232 | tf_op jit(solution)/shard_map/all_gather | solution.py:106
  186.6 175.9 %while.26 = (s32[]{:T(128)}, f32[32,2,64,256]{3,2,1,0:T(8,128)}, bf16[32,2048,128]{2,1,0:T(8,128)(2,1)}, bf16[2048,256]{1,0:T(8,128)(2,1)}, s32[]{:T(128)}, /*in...) while((s32[]{:T(128)}, f32[32,2,64,256]{3,2,1,0:T(8,128)}, ...), condition=%wide.region_5.6_spmd, body=%wide.region_4.5_spmd.sunk | while | flops 134742032 | bytes 10027344 | solution.py:122
  189.5 2.6 bitcast_dynamic-update-slice_fusion.2
  195.0 2.6 bitcast_dynamic-update-slice_fusion.2
  200.5 2.6 bitcast_dynamic-update-slice_fusion.2
  206.0 2.6 bitcast_dynamic-update-slice_fusion.2
  211.5 2.6 bitcast_dynamic-update-slice_fusion.2
  216.9 2.6 bitcast_dynamic-update-slice_fusion.2
  222.4 2.6 bitcast_dynamic-update-slice_fusion.2
  227.9 2.6 bitcast_dynamic-update-slice_fusion.2
  233.4 2.6 bitcast_dynamic-update-slice_fusion.2
  238.9 2.6 bitcast_dynamic-update-slice_fusion.2
  244.4 2.6 bitcast_dynamic-update-slice_fusion.2
  249.9 2.6 bitcast_dynamic-update-slice_fusion.2
  255.4 2.6 bitcast_dynamic-update-slice_fusion.2
  260.9 2.6 bitcast_dynamic-update-slice_fusion.2
  266.4 2.6 bitcast_dynamic-update-slice_fusion.2
  271.9 2.6 bitcast_dynamic-update-slice_fusion.2
  277.4 2.6 bitcast_dynamic-update-slice_fusion.2
  288.4 2.6 bitcast_dynamic-update-slice_fusion.2
  293.9 2.6 bitcast_dynamic-update-slice_fusion.2
  299.4 2.6 bitcast_dynamic-update-slice_fusion.2
  304.9 2.6 bitcast_dynamic-update-slice_fusion.2
  310.4 2.6 bitcast_dynamic-update-slice_fusion.2
  315.9 2.6 bitcast_dynamic-update-slice_fusion.2
  321.4 2.6 bitcast_dynamic-update-slice_fusion.2
  326.9 2.6 bitcast_dynamic-update-slice_fusion.2
  332.4 2.6 bitcast_dynamic-update-slice_fusion.2
  337.9 2.6 bitcast_dynamic-update-slice_fusion.2
  343.4 2.6 bitcast_dynamic-update-slice_fusion.2
  348.9 2.6 bitcast_dynamic-update-slice_fusion.2
  354.4 2.6 bitcast_dynamic-update-slice_fusion.2
  359.9 2.6 bitcast_dynamic-update-slice_fusion.2
  362.5 100.2 %all-reduce.1 = bf16[4096,256]{1,0:T(8,128)(2,1)S(1)} all-reduce(f32[4096,256]{1,0:T(8,128)} %bitcast.62), channel_id=1, replica_groups=mesh['tp'=2,'sp'=32,'dp'=4] {'tp'}, use_global_device_ids=true, to_apply=%region_6.7 | all-reduce | flops 1048576 | bytes 6291456 | tf_op jit(solution)/shard_map/psum | solution.py:125
  464.4 64.7 %psum.15 = f32[2048]{0:T(1024)S(1)} all-reduce(f32[2048]{0:T(1024)S(1)} %get-tuple-element.206), channel_id=1, replica_groups=mesh['tp'=2,'sp'=32,'dp'=4] {'sp'}, use_global_device_ids=true, to_apply=%region_8.9 | all-reduce | flops 2048 | bytes 16384 | tf_op jit(solution)/shard_map/psum | solution.py:130
  (104 shorter events, 109.9 us)
Async XLA Ops:
  7.2 11.8 %copy-start.2 = (s32[4096]{0:T(1024)S(1)}, s32[4096]{0:T(1024)}, u32[]{:S(2)}) copy-start(s32[4096]{0:T(1024)} %param.15) | copy-start | bytes 49156
  7.2 12.0 %copy-start.1 = (bf16[128,2048]{1,0:T(8,128)(2,1)S(1)}, bf16[128,2048]{1,0:T(8,128)(2,1)}, u32[]{:S(2)}) copy-start(bf16[128,2048]{1,0:T(8,128)(2,1)} %param.12) | copy-start | bytes 1572868
  7.2 66.2 %all-gather.3.cloned.1.call-start = ((), (), s32[]{:S(2)}) async-start(), calls=%async_computation.2 | async-start | bytes 2162688 | tf_op jit(solution)/shard_map/all_gather | solution.py:78
  10.3 37.9 %all-to-all-start.1 = ((bf16[32,128,256]{2,1,0:T(8,128)(2,1)}), bf16[32,128,256]{2,1,0:T(8,128)(2,1)S(1)}, u32[]{:S(2)}, u32[]{:S(2)}) async-start(bf16[32,128,256]{2,1,0:T(8,128)(2,1)} %tile.2), calls=%async_computation.1 | async-start | bytes 4194304 | tf_op jit(solution)/shard_map/all_to_all | solution.py:17
  48.2 26.5 %all-to-all-start = ((bf16[32,64,128]{2,1,0:T(8,128)(2,1)}), bf16[32,64,128]{2,1,0:T(8,128)(2,1)}, u32[]{:S(2)}, u32[]{:S(2)}) async-start(bf16[32,64,128]{2,1,0:T(8,128)(2,1)} %bitcast.4), calls=%async_computation | async-start | bytes 1048576 | tf_op jit(solution)/shard_map/all_to_all | solution.py:76
  53.2 131.0 %all-gather.5.cloned.1.call-start = ((), (), s32[]{:S(2)}) async-start(), calls=%async_computation.3 | async-start | bytes 17301504 | tf_op jit(solution)/shard_map/all_gather | solution.py:106
  74.7 31.0 %copy-start.4 = (s32[256]{0:T(256)S(1)}, s32[256]{0:T(256)}, u32[]{:S(2)}) copy-start(s32[256]{0:T(256)} %param.19) | copy-start | bytes 3076
  362.5 166.6 %copy-start.3 = (f32[256]{0:T(256)S(1)}, f32[256]{0:T(256)}, u32[]{:S(2)}) copy-start(f32[256]{0:T(256)} %param.18) | copy-start | bytes 3076
  464.4 66.2 %copy-start = (bf16[2048,256]{1,0:T(8,128)(2,1)}, bf16[2048,256]{1,0:T(8,128)(2,1)S(1)}, u32[]{:S(2)}) copy-start(bf16[2048,256]{1,0:T(8,128)(2,1)S(1)} %get-tuple-element.207) | copy-start | bytes 3145732
Sparse Core Ops, SparseCore 0:
  10.5 62.7 all-gather.2
  105.8 78.3 all-gather.4
